TPU v7x, 32 devices: a whole 2x2x4 slice. The times are simulated.
32 devices in a mesh: dom: 8 (over z, core), rep: 4 (over y, x).
Axes of the slice: x: 2, y: 2, z: 4, core: 2. Of those that a mesh axis runs over, the one named last changes fastest.
Arguments:
- node_features: bfloat16 [16384, 256], P(('dom', 'rep')), may hold values from -6 to 6
- weight: bfloat16 [256, 256], replicated, may hold values from -0.375 to 0.375
- cotangent: bfloat16 [16384, 256], P(('dom', 'rep')), may hold values from -6 to 6
- tile_row: int32 [8, 4, 512], P('dom', 'rep'), may hold values from 0 to 15
- tile_col: int32 [8, 4, 512], P('dom', 'rep'), may hold values from 0 to 31
- tile_values: bfloat16 [8, 4, 512, 128, 128], P('dom', 'rep'), may hold values from -0.0625 to 0.0625
- tile_count: int32 [8, 4], P('dom', 'rep'), may hold values from 128 to 512, as said below
Outputs:
- output: bfloat16 [16384, 256], P(('dom', 'rep'))
- grad_features: bfloat16 [16384, 256], P(('dom', 'rep'))
- grad_weight: float32 [256, 256], replicated
Inputs may be any that keep to these rules, and one draw needn't show every extreme that they name: Live slots are the first tile_count slots of each device's list; some device has all 512 slots live.
All inputs are finite; a program needn't handle non-finite values.
Results may differ from a plain program's by a relative error of at most 0.0061.
Values may be sent and summed in bfloat16 or wider, within the bound.
A program may use at most 192 MiB of HBM per device.

v0:
```python
import jax
import jax.numpy as jnp
from jax import lax
from jax.sharding import PartitionSpec as P


def silu_slope(summed):
    sig = jax.nn.sigmoid(summed)
    return sig * (1.0 + summed * (1.0 - sig))


def tile_products(values, pick_index, place_index, active, source, out_blocks, flipped):
    slots = values.shape[0]
    feature_width = source.shape[2]
    per_turn = min(slots, 128)
    pattern = "tba,tbf->taf" if flipped else "tab,tbf->taf"

    def accumulate(turn_index, summed):
        first_slot = turn_index * per_turn
        block_values = lax.dynamic_slice_in_dim(values, first_slot, per_turn, 0)
        picks = lax.dynamic_slice_in_dim(pick_index, first_slot, per_turn, 0)
        picked = jnp.take(source, picks, axis=0)
        products = jnp.einsum(pattern, block_values, picked, preferred_element_type=jnp.float32)
        places = lax.dynamic_slice_in_dim(place_index, first_slot, per_turn, 0)
        enabled = lax.dynamic_slice_in_dim(active, first_slot, per_turn, 0)
        products = products * enabled.astype(jnp.float32)[:, None, None]
        return summed.at[places].add(products)

    initial = jnp.zeros((out_blocks, 128, feature_width), jnp.float32)
    summed = lax.fori_loop(0, slots // per_turn, accumulate, initial)
    return summed.reshape(out_blocks * 128, feature_width)


def body(node_features, weight, cotangent, tile_row, tile_col, tile_values, tile_count):
    rows_here = node_features.shape[0]
    feature_width = weight.shape[0]
    dom_size = lax.axis_size("dom")
    rep_size = lax.axis_size("rep")
    slots = tile_row.shape[2]
    row_index = tile_row.reshape(slots)
    col_index = tile_col.reshape(slots)
    values = tile_values.reshape(slots, 128, 128)
    active = lax.broadcasted_iota(jnp.int32, (slots,), 0) < tile_count.reshape(())
    raw_rows = lax.all_gather(node_features, "dom", axis=0, tiled=True)
    gathered = jnp.dot(raw_rows, weight, preferred_element_type=jnp.float32).astype(jnp.bfloat16)
    source = gathered.reshape(-1, 128, feature_width)
    part_blocks = rep_size * rows_here // 128
    partial_value = tile_products(values, col_index, row_index, active, source, part_blocks, False)
    summed = lax.psum_scatter(partial_value, "rep", scatter_dimension=0, tiled=True)
    output = jax.nn.silu(summed).astype(jnp.bfloat16)
    grad_own = (cotangent.astype(jnp.float32) * silu_slope(summed)).astype(jnp.bfloat16)
    grad_block = lax.all_gather(grad_own, "rep", axis=0, tiled=True)
    back_blocks = dom_size * rows_here // 128
    back_partial = tile_products(
        values,
        row_index,
        col_index,
        active,
        grad_block.reshape(-1, 128, feature_width),
        back_blocks,
        True,
    )
    grad_projected = lax.psum_scatter(back_partial, "dom", scatter_dimension=0, tiled=True).astype(
        jnp.bfloat16
    )
    grad_features = jnp.dot(grad_projected, weight.T, preferred_element_type=jnp.float32).astype(
        jnp.bfloat16
    )
    local_weight = jnp.dot(node_features.T, grad_projected, preferred_element_type=jnp.float32)
    grad_weight = lax.psum(local_weight, ("dom", "rep"))
    return (output, grad_features, grad_weight)


def solution(mesh):
    placed = (
        P(("dom", "rep"), None),
        P(),
        P(("dom", "rep"), None),
        P("dom", "rep", None),
        P("dom", "rep", None),
        P("dom", "rep", None, None, None),
        P("dom", "rep"),
    )
    return jax.shard_map(
        body,
        mesh=mesh,
        in_specs=placed,
        out_specs=(P(("dom", "rep"), None), P(("dom", "rep"), None), P()),
        check_vma=False,
    )
```

profile of v0, /device:TPU:0, one launch (start us, length us, event | category | flops | bytes accessed | tf_op | source)
XLA Modules:
  0.0 718.8 jit_solution(10474179831010498034)
XLA Ops:
  7.2 0.7 all-gather.3.cloned.1.call-update
  8.6 32.9 %all-gather.3.cloned.1.call-done = bf16[4096,256]{1,0:T(8,128)(2,1)} async-done(((bf16[512,256]{1,0:T(8,128)(2,1)}), bf16[4096,256]{1,0:T(8,128)(2,1)}) %all-gather.3.cloned.1.call-update) | async-done | bytes 2097168 | tf_op jit(solution)/shard_map/all_gather | solution.py:44
  41.5 3.7 convolution_convert_fusion
  45.2 0.2 broadcast_in_dim.74
  45.4 182.0 %while.26 = (s32[]{:T(128)}, f32[16,128,256]{2,1,0:T(8,128)S(1)}, s32[512]{0:T(512)S(1)}, bf16[512,128,128]{2,1,0:T(8,128)(2,1)}, s32[512]{0:T(512)S(1)}, /*inde...) while((s32[]{:T(128)}, f32[16,128,256]{2,1,0:T(8,128)S(1)}, ...), condition=%wide.region_2.3_spmd, body=%wide.region_0.2_spmd.sunk | while | flops 1086327040 | bytes 96478248 | solution.py:30
  45.4 0.1 compare_and_fusion.4
  45.5 8.2 %gather_fusion = bf16[128,128,256]{2,1,0:T(8,128)(2,1)} fusion(bf16[32,128,256]{2,1,0:T(8,128)(2,1)} %get-tuple-element.424, s32[1024]{0:T(1024)S(1)} %pad_clamp_fusion.4), kind=kCustom, calls=%fused_computation.clone.1 | custom fusion | bytes 16777728 | tf_op jit(solution)/shard_map/while/body/eval_jaxpr/jit(_take)/gather | solution.py:22
  53.7 12.8 %convolution_multiply_fusion.4 = f32[128,128,256]{2,1,0:T(8,128)} fusion(f32[128]{0:T(128)S(1)} %get-tuple-element.384, bf16[128,128,256]{2,1,0:T(8,128)(2,1)} %gather_fusion, pred[128]{0:T(512)(128)(4,1)S(1)} %get-tuple-element.386, bf16[512,128,128]{2,1,0:T(8,128)(2,1)} %get-tuple-element.422, s32[]{:T(128)S(6)} %select_n.85), kind=kOutput, calls=%fused_computation.4.clone.1 | convolution fusion | flops 1082130432 | bytes 29360772 | tf_op jit(solution)/shard_map/while/body/eval_jaxpr/tab,tbf->taf/dot_general | solution.py:23
  66.6 24.3 %scatter_fusion = f32[16,128,256]{2,1,0:T(8,128)S(1)} fusion(f32[16,128,256]{2,1,0:T(8,128)S(1)} %get-tuple-element.409, s32[128]{0:T(128)S(1)} %compare_select_fusion.8, f32[128,128,256]{2,1,0:T(8,128)} %convolution_multiply_fusion.4), kind=kCustom, calls=%fused_computation.2.clone.1 | custom fusion | flops 4194304 | bytes 50332160 | tf_op jit(solution)/shard_map/while/body/eval_jaxpr/scatter-add | solution.py:27
  90.9 0.1 compare_and_fusion.4
  91.0 8.2 %gather_fusion = bf16[128,128,256]{2,1,0:T(8,128)(2,1)} fusion(bf16[32,128,256]{2,1,0:T(8,128)(2,1)} %get-tuple-element.424, s32[1024]{0:T(1024)S(1)} %pad_clamp_fusion.4), kind=kCustom, calls=%fused_computation.clone.1 | custom fusion | bytes 16777728 | tf_op jit(solution)/shard_map/while/body/eval_jaxpr/jit(_take)/gather | solution.py:22
  99.2 12.8 %convolution_multiply_fusion.4 = f32[128,128,256]{2,1,0:T(8,128)} fusion(f32[128]{0:T(128)S(1)} %get-tuple-element.384, bf16[128,128,256]{2,1,0:T(8,128)(2,1)} %gather_fusion, pred[128]{0:T(512)(128)(4,1)S(1)} %get-tuple-element.386, bf16[512,128,128]{2,1,0:T(8,128)(2,1)} %get-tuple-element.422, s32[]{:T(128)S(6)} %select_n.85), kind=kOutput, calls=%fused_computation.4.clone.1 | convolution fusion | flops 1082130432 | bytes 29360772 | tf_op jit(solution)/shard_map/while/body/eval_jaxpr/tab,tbf->taf/dot_general | solution.py:23
  112.1 24.3 %scatter_fusion = f32[16,128,256]{2,1,0:T(8,128)S(1)} fusion(f32[16,128,256]{2,1,0:T(8,128)S(1)} %get-tuple-element.409, s32[128]{0:T(128)S(1)} %compare_select_fusion.8, f32[128,128,256]{2,1,0:T(8,128)} %convolution_multiply_fusion.4), kind=kCustom, calls=%fused_computation.2.clone.1 | custom fusion | flops 4194304 | bytes 50332160 | tf_op jit(solution)/shard_map/while/body/eval_jaxpr/scatter-add | solution.py:27
  136.4 0.1 compare_and_fusion.4
  136.5 8.2 %gather_fusion = bf16[128,128,256]{2,1,0:T(8,128)(2,1)} fusion(bf16[32,128,256]{2,1,0:T(8,128)(2,1)} %get-tuple-element.424, s32[1024]{0:T(1024)S(1)} %pad_clamp_fusion.4), kind=kCustom, calls=%fused_computation.clone.1 | custom fusion | bytes 16777728 | tf_op jit(solution)/shard_map/while/body/eval_jaxpr/jit(_take)/gather | solution.py:22
  144.7 12.8 %convolution_multiply_fusion.4 = f32[128,128,256]{2,1,0:T(8,128)} fusion(f32[128]{0:T(128)S(1)} %get-tuple-element.384, bf16[128,128,256]{2,1,0:T(8,128)(2,1)} %gather_fusion, pred[128]{0:T(512)(128)(4,1)S(1)} %get-tuple-element.386, bf16[512,128,128]{2,1,0:T(8,128)(2,1)} %get-tuple-element.422, s32[]{:T(128)S(6)} %select_n.85), kind=kOutput, calls=%fused_computation.4.clone.1 | convolution fusion | flops 1082130432 | bytes 29360772 | tf_op jit(solution)/shard_map/while/body/eval_jaxpr/tab,tbf->taf/dot_general | solution.py:23
  157.6 24.3 %scatter_fusion = f32[16,128,256]{2,1,0:T(8,128)S(1)} fusion(f32[16,128,256]{2,1,0:T(8,128)S(1)} %get-tuple-element.409, s32[128]{0:T(128)S(1)} %compare_select_fusion.8, f32[128,128,256]{2,1,0:T(8,128)} %convolution_multiply_fusion.4), kind=kCustom, calls=%fused_computation.2.clone.1 | custom fusion | flops 4194304 | bytes 50332160 | tf_op jit(solution)/shard_map/while/body/eval_jaxpr/scatter-add | solution.py:27
  181.9 0.1 compare_and_fusion.4
  182.0 8.2 %gather_fusion = bf16[128,128,256]{2,1,0:T(8,128)(2,1)} fusion(bf16[32,128,256]{2,1,0:T(8,128)(2,1)} %get-tuple-element.424, s32[1024]{0:T(1024)S(1)} %pad_clamp_fusion.4), kind=kCustom, calls=%fused_computation.clone.1 | custom fusion | bytes 16777728 | tf_op jit(solution)/shard_map/while/body/eval_jaxpr/jit(_take)/gather | solution.py:22
  190.2 12.8 %convolution_multiply_fusion.4 = f32[128,128,256]{2,1,0:T(8,128)} fusion(f32[128]{0:T(128)S(1)} %get-tuple-element.384, bf16[128,128,256]{2,1,0:T(8,128)(2,1)} %gather_fusion, pred[128]{0:T(512)(128)(4,1)S(1)} %get-tuple-element.386, bf16[512,128,128]{2,1,0:T(8,128)(2,1)} %get-tuple-element.422, s32[]{:T(128)S(6)} %select_n.85), kind=kOutput, calls=%fused_computation.4.clone.1 | convolution fusion | flops 1082130432 | bytes 29360772 | tf_op jit(solution)/shard_map/while/body/eval_jaxpr/tab,tbf->taf/dot_general | solution.py:23
  203.1 24.3 %scatter_fusion = f32[16,128,256]{2,1,0:T(8,128)S(1)} fusion(f32[16,128,256]{2,1,0:T(8,128)S(1)} %get-tuple-element.409, s32[128]{0:T(128)S(1)} %compare_select_fusion.8, f32[128,128,256]{2,1,0:T(8,128)} %convolution_multiply_fusion.4), kind=kCustom, calls=%fused_computation.2.clone.1 | custom fusion | flops 4194304 | bytes 50332160 | tf_op jit(solution)/shard_map/while/body/eval_jaxpr/scatter-add | solution.py:27
  227.4 1.3 copy-done.1
  228.8 34.7 %reduce-scatter.3.cloned.1.call-done = f32[512,256]{1,0:T(8,128)} async-done(((f32[2048,256]{1,0:T(8,128)}), f32[512,256]{1,0:T(8,128)}) %reduce-scatter.3.cloned.1.call-update) | async-done | bytes 524304 | tf_op jit(solution)/shard_map/reduce_scatter | solution.py:49
  263.5 2.1 multiply_convert_fusion
  265.6 0.2 reduce-scatter.5.cloned.1.call-start
  265.8 22.4 %copy.10 = bf16[1,1,512,128,128]{3,4,2,1,0:T(8,128)(2,1)} copy(bf16[1,1,512,128,128]{4,3,2,1,0:T(8,128)(2,1)} %bitcast.21) | data formatting | bytes 33554432 | tf_op args[5]
  288.2 4.2 all-gather.5.cloned.1.call-done
  292.4 2.4 broadcast_in_dim.75
  294.8 234.0 %while.27 = (s32[]{:T(128)}, f32[32,128,256]{2,1,0:T(8,128)}, s32[512]{0:T(512)S(1)}, bf16[512,128,128]{1,2,0:T(8,128)(2,1)}, s32[512]{0:T(512)S(1)}, /*index=5*...) while((s32[]{:T(128)}, f32[32,128,256]{2,1,0:T(8,128)}, ...), condition=%wide.region_6.7_spmd, body=%wide.region_4.6_spmd.sunk | while | flops 1086327040 | bytes 96478248 | solution.py:30
  294.8 0.1 compare_and_fusion.5
  294.9 7.7 %gather_fusion.1 = bf16[128,128,256]{2,1,0:T(8,128)(2,1)} fusion(bf16[16,128,256]{2,1,0:T(8,128)(2,1)} %get-tuple-element.457, s32[1024]{0:T(1024)S(1)} %pad_clamp_fusion.5), kind=kCustom, calls=%fused_computation.1.clone.1 | custom fusion | bytes 16777728 | tf_op jit(solution)/shard_map/while/body/eval_jaxpr/jit(_take)/gather | solution.py:22
  302.7 12.8 %convolution_multiply_fusion.5 = f32[128,128,256]{2,1,0:T(8,128)} fusion(f32[128]{0:T(128)S(1)} %get-tuple-element.394, bf16[128,128,256]{2,1,0:T(8,128)(2,1)} %gather_fusion.1, pred[128]{0:T(512)(128)(4,1)S(1)} %get-tuple-element.396, bf16[512,128,128]{1,2,0:T(8,128)(2,1)} %get-tuple-element.455, s32[]{:T(128)S(6)} %select_n.88), kind=kOutput, calls=%fused_computation.16.clone.1 | convolution fusion | flops 1082130432 | bytes 29360772 | tf_op jit(solution)/shard_map/while/body/eval_jaxpr/tba,tbf->taf/dot_general | solution.py:23
  315.6 37.8 %scatter_fusion.1 = f32[32,128,256]{2,1,0:T(8,128)} fusion(f32[32,128,256]{2,1,0:T(8,128)} %get-tuple-element.442, s32[128]{0:T(128)S(1)} %compare_select_fusion.9, f32[128,128,256]{2,1,0:T(8,128)} %convolution_multiply_fusion.5), kind=kCustom, calls=%fused_computation.3.clone.1 | custom fusion | flops 4194304 | bytes 50332160 | tf_op jit(solution)/shard_map/while/body/eval_jaxpr/scatter-add | solution.py:27
  353.4 0.1 compare_and_fusion.5
  353.5 7.7 %gather_fusion.1 = bf16[128,128,256]{2,1,0:T(8,128)(2,1)} fusion(bf16[16,128,256]{2,1,0:T(8,128)(2,1)} %get-tuple-element.457, s32[1024]{0:T(1024)S(1)} %pad_clamp_fusion.5), kind=kCustom, calls=%fused_computation.1.clone.1 | custom fusion | bytes 16777728 | tf_op jit(solution)/shard_map/while/body/eval_jaxpr/jit(_take)/gather | solution.py:22
  361.2 12.8 %convolution_multiply_fusion.5 = f32[128,128,256]{2,1,0:T(8,128)} fusion(f32[128]{0:T(128)S(1)} %get-tuple-element.394, bf16[128,128,256]{2,1,0:T(8,128)(2,1)} %gather_fusion.1, pred[128]{0:T(512)(128)(4,1)S(1)} %get-tuple-element.396, bf16[512,128,128]{1,2,0:T(8,128)(2,1)} %get-tuple-element.455, s32[]{:T(128)S(6)} %select_n.88), kind=kOutput, calls=%fused_computation.16.clone.1 | convolution fusion | flops 1082130432 | bytes 29360772 | tf_op jit(solution)/shard_map/while/body/eval_jaxpr/tba,tbf->taf/dot_general | solution.py:23
  374.1 37.8 %scatter_fusion.1 = f32[32,128,256]{2,1,0:T(8,128)} fusion(f32[32,128,256]{2,1,0:T(8,128)} %get-tuple-element.442, s32[128]{0:T(128)S(1)} %compare_select_fusion.9, f32[128,128,256]{2,1,0:T(8,128)} %convolution_multiply_fusion.5), kind=kCustom, calls=%fused_computation.3.clone.1 | custom fusion | flops 4194304 | bytes 50332160 | tf_op jit(solution)/shard_map/while/body/eval_jaxpr/scatter-add | solution.py:27
  412.0 7.8 %gather_fusion.1 = bf16[128,128,256]{2,1,0:T(8,128)(2,1)} fusion(bf16[16,128,256]{2,1,0:T(8,128)(2,1)} %get-tuple-element.457, s32[1024]{0:T(1024)S(1)} %pad_clamp_fusion.5), kind=kCustom, calls=%fused_computation.1.clone.1 | custom fusion | bytes 16777728 | tf_op jit(solution)/shard_map/while/body/eval_jaxpr/jit(_take)/gather | solution.py:22
  419.8 12.8 %convolution_multiply_fusion.5 = f32[128,128,256]{2,1,0:T(8,128)} fusion(f32[128]{0:T(128)S(1)} %get-tuple-element.394, bf16[128,128,256]{2,1,0:T(8,128)(2,1)} %gather_fusion.1, pred[128]{0:T(512)(128)(4,1)S(1)} %get-tuple-element.396, bf16[512,128,128]{1,2,0:T(8,128)(2,1)} %get-tuple-element.455, s32[]{:T(128)S(6)} %select_n.88), kind=kOutput, calls=%fused_computation.16.clone.1 | convolution fusion | flops 1082130432 | bytes 29360772 | tf_op jit(solution)/shard_map/while/body/eval_jaxpr/tba,tbf->taf/dot_general | solution.py:23
  432.7 37.7 %scatter_fusion.1 = f32[32,128,256]{2,1,0:T(8,128)} fusion(f32[32,128,256]{2,1,0:T(8,128)} %get-tuple-element.442, s32[128]{0:T(128)S(1)} %compare_select_fusion.9, f32[128,128,256]{2,1,0:T(8,128)} %convolution_multiply_fusion.5), kind=kCustom, calls=%fused_computation.3.clone.1 | custom fusion | flops 4194304 | bytes 50332160 | tf_op jit(solution)/shard_map/while/body/eval_jaxpr/scatter-add | solution.py:27
  470.4 7.8 %gather_fusion.1 = bf16[128,128,256]{2,1,0:T(8,128)(2,1)} fusion(bf16[16,128,256]{2,1,0:T(8,128)(2,1)} %get-tuple-element.457, s32[1024]{0:T(1024)S(1)} %pad_clamp_fusion.5), kind=kCustom, calls=%fused_computation.1.clone.1 | custom fusion | bytes 16777728 | tf_op jit(solution)/shard_map/while/body/eval_jaxpr/jit(_take)/gather | solution.py:22
  478.2 12.8 %convolution_multiply_fusion.5 = f32[128,128,256]{2,1,0:T(8,128)} fusion(f32[128]{0:T(128)S(1)} %get-tuple-element.394, bf16[128,128,256]{2,1,0:T(8,128)(2,1)} %gather_fusion.1, pred[128]{0:T(512)(128)(4,1)S(1)} %get-tuple-element.396, bf16[512,128,128]{1,2,0:T(8,128)(2,1)} %get-tuple-element.455, s32[]{:T(128)S(6)} %select_n.88), kind=kOutput, calls=%fused_computation.16.clone.1 | convolution fusion | flops 1082130432 | bytes 29360772 | tf_op jit(solution)/shard_map/while/body/eval_jaxpr/tba,tbf->taf/dot_general | solution.py:23
  491.1 37.8 %scatter_fusion.1 = f32[32,128,256]{2,1,0:T(8,128)} fusion(f32[32,128,256]{2,1,0:T(8,128)} %get-tuple-element.442, s32[128]{0:T(128)S(1)} %compare_select_fusion.9, f32[128,128,256]{2,1,0:T(8,128)} %convolution_multiply_fusion.5), kind=kCustom, calls=%fused_computation.3.clone.1 | custom fusion | flops 4194304 | bytes 50332160 | tf_op jit(solution)/shard_map/while/body/eval_jaxpr/scatter-add | solution.py:27
  529.0 50.6 %reduce-scatter.5.cloned.1.call-done = f32[512,256]{1,0:T(8,128)} async-done(((f32[4096,256]{1,0:T(8,128)}), f32[512,256]{1,0:T(8,128)}) %reduce-scatter.5.cloned.1.call-update) | async-done | bytes 524304 | tf_op jit(solution)/shard_map/reduce_scatter | solution.py:63
  579.5 2.0 convolution_bitcast_fusion
  581.6 2.0 convolution_convert_fusion.1
  583.6 126.9 %all-reduce.2.cloned.1.call-done = f32[256,256]{0,1:T(8,128)} async-done(((f32[256,256]{0,1:T(8,128)}), f32[256,256]{0,1:T(8,128)}) %all-reduce.2.cloned.1.call-update) | async-done | bytes 262160 | tf_op jit(solution)/shard_map/psum | solution.py:70
  710.5 1.8 copy.12
  (38 shorter events, 1.1 us)
Async XLA Ops:
  7.2 34.4 %copy-start = (bf16[256,256]{1,0:T(8,128)(2,1)S(1)}, bf16[256,256]{1,0:T(8,128)(2,1)}, u32[]{:S(2)}) copy-start(bf16[256,256]{1,0:T(8,128)(2,1)} %param.12) | copy-start | bytes 393220
  7.2 38.2 %copy-start.4 = (s32[1,1,512]{2,1,0:T(1,128)S(1)}, s32[1,1,512]{2,1,0:T(1,128)}, u32[]{:S(2)}) copy-start(s32[1,1,512]{2,1,0:T(1,128)} %param.14) | copy-start | bytes 6148
  7.2 38.2 %copy-start.5 = (s32[1,1,512]{2,1,0:T(1,128)S(1)}, s32[1,1,512]{2,1,0:T(1,128)}, u32[]{:S(2)}) copy-start(s32[1,1,512]{2,1,0:T(1,128)} %param.15) | copy-start | bytes 6148
  7.2 34.3 %all-gather.3.cloned.1.call-start = ((), (), s32[]{:S(2)}) async-start(), calls=%async_computation.2 | async-start | bytes 2359296 | tf_op jit(solution)/shard_map/all_gather | solution.py:44
  7.9 255.5 %reduce-scatter.3.cloned.1.call-start = ((), (), s32[]{:S(2)}) async-start(), calls=%async_computation.3 | async-start | bytes 2621440 | tf_op jit(solution)/shard_map/reduce_scatter | solution.py:49
  45.4 218.1 %copy-start.3 = (bf16[512,256]{1,0:T(8,128)(2,1)S(1)}, bf16[512,256]{1,0:T(8,128)(2,1)}, u32[]{:S(2)}) copy-start(bf16[512,256]{1,0:T(8,128)(2,1)} %param.13) | copy-start | bytes 786436
  227.4 1.3 copy-start.1
  228.8 63.7 %all-gather.5.cloned.1.call-start = ((), (), s32[]{:S(2)}) async-start(), calls=%async_computation.4 | async-start | bytes 1310720 | tf_op jit(solution)/shard_map/all_gather | solution.py:52
  265.6 314.0 %reduce-scatter.5.cloned.1.call-start = ((), (), s32[]{:S(2)}) async-start(), calls=%async_computation.5 | async-start | bytes 4718592 | tf_op jit(solution)/shard_map/reduce_scatter | solution.py:63
  294.8 284.7 %copy-start.2 = (bf16[512,256]{1,0:T(8,128)(2,1)S(1)}, bf16[512,256]{1,0:T(8,128)(2,1)}, u32[]{:S(2)}) copy-start(bf16[512,256]{1,0:T(8,128)(2,1)} %param.11) | copy-start | bytes 786436
  528.9 181.6 %all-reduce.2.cloned.1.call-start = ((), (), s32[]{:S(2)}) async-start(), calls=%async_computation.6 | async-start | bytes 524288 | tf_op jit(solution)/shard_map/psum | solution.py:70
Sparse Core Ops, SparseCore 0:
  9.6 31.8 all-gather.2
  228.9 34.5 reduce-scatter.2
  265.9 26.4 all-gather.4
  529.0 50.4 reduce-scatter.4
  585.5 125.0 all-reduce.1
where the time goes:
time: 721 us; the launch traced here: 719 us
  other arithmetic  252 us (35%)
  waiting for transfers between devices  250 us (35%)
  matrix products  110 us (15%)
  local copies, waits for them, and re-layouts  91.8 us (13%)
  between operations  14.5 us (2%)
    scatter-add x8, other arithmetic, accumulate(): return summed.at[places].add(products)  248 us
    psum x1, waiting for transfers between devices, body(): grad_weight = lax.psum(local_weight, ('dom', 'rep'))  127 us
    dot_general x8, matrix products, accumulate(): jnp.einsum(pattern, block_values, picked, preferred_element_type=jnp.floa...  103 us
    gather x8, local copies, waits for them, and re-layouts, accumulate(): picked = jnp.take(source, picks, axis=0)  63.7 us
    reduce_scatter x1, waiting for transfers between devices, body(): lax.psum_scatter(back_partial, 'dom', scatter_dimension=0, tiled=True)  50.6 us
    reduce_scatter x1, waiting for transfers between devices, body(): lax.psum_scatter(partial_value, 'rep', scatter_dimension=0, tiled=True)  34.7 us
    all_gather x1, waiting for transfers between devices, body(): raw_rows = lax.all_gather(node_features, 'dom', axis=0, tiled=True)  32.9 us
    unnamed x14, local copies, waits for them, and re-layouts  25.5 us
  transfers between devices with their start and end apart: 5, of which 5 were waited for; matrix products, arithmetic and copies ran while one was open for 3% of the time, Pallas kernels for 0%

commit v1 on v0

v1 whole, which is shorter than its diff:
```python
import functools

import jax
import jax.numpy as jnp
from jax import lax
from jax.experimental import pallas as pl
from jax.experimental.pallas import tpu as pltpu
from jax.sharding import PartitionSpec as P

CHUNKS = 8


def build_kernel(row_blocks, col_blocks, row_ref, col_ref, count_ref, tiles_ref, dense_ref, tiles, stage, head, after, in_sem, out_sem):
    slots = tiles.shape[0]
    per_chunk = slots // CHUNKS
    count = count_ref[0]
    loads = [
        pltpu.make_async_copy(
            tiles_ref.at[pl.ds(c * per_chunk, per_chunk)],
            tiles.at[pl.ds(c * per_chunk, per_chunk)],
            in_sem.at[c],
        )
        for c in range(CHUNKS)
    ]
    for c in range(CHUNKS):
        loads[c].start()

    def clear(p, carry):
        for u in range(8):
            head[p * 8 + u] = -1
        return carry

    lax.fori_loop(0, row_blocks * col_blocks // 8, clear, 0)

    def link(k, carry):
        place = row_ref[k] * col_blocks + col_ref[k]
        after[k] = head[place]
        head[place] = k
        return carry

    lax.fori_loop(0, count, link, 0)
    for c in range(CHUNKS):
        loads[c].wait()

    def out_copy(rb):
        slot = lax.rem(rb, 2)
        return pltpu.make_async_copy(
            stage.at[slot], dense_ref.at[pl.ds(pl.multiple_of(rb * 128, 128), 128)], out_sem.at[slot]
        )

    def one_row(rb, carry):
        slot = lax.rem(rb, 2)

        @pl.when(rb >= 2)
        def _():
            out_copy(rb - 2).wait()

        def one_place(cb, inner):
            first = head[rb * col_blocks + cb]
            start = jnp.maximum(first, 0)
            value = tiles[start].astype(jnp.float32)
            value = jnp.where(first >= 0, value, 0.0)
            follow = jnp.where(first >= 0, after[start], -1)

            def more(state):
                return state[0] >= 0

            def add(state):
                k, total = state
                return after[k], total + tiles[k].astype(jnp.float32)

            unused, value = lax.while_loop(more, add, (follow, value))
            stage[slot, :, pl.ds(pl.multiple_of(cb * 128, 128), 128)] = value.astype(jnp.bfloat16)
            return inner

        lax.fori_loop(0, col_blocks, one_place, 0)
        out_copy(rb).start()
        return carry

    lax.fori_loop(0, row_blocks, one_row, 0)
    out_copy(row_blocks - 2).wait()
    out_copy(row_blocks - 1).wait()


def build_dense(row_index, col_index, count, values, row_blocks, col_blocks):
    slots = values.shape[0]
    smem = pl.BlockSpec(memory_space=pltpu.SMEM)
    return pl.pallas_call(
        functools.partial(build_kernel, row_blocks, col_blocks),
        out_shape=jax.ShapeDtypeStruct((row_blocks * 128, col_blocks * 128), jnp.bfloat16),
        in_specs=[smem, smem, smem, pl.BlockSpec(memory_space=pl.ANY)],
        out_specs=pl.BlockSpec(memory_space=pl.ANY),
        scratch_shapes=[
            pltpu.VMEM((slots, 128, 128), jnp.bfloat16),
            pltpu.VMEM((2, 128, col_blocks * 128), jnp.bfloat16),
            pltpu.SMEM((row_blocks * col_blocks,), jnp.int32),
            pltpu.SMEM((slots,), jnp.int32),
            pltpu.SemaphoreType.DMA((CHUNKS,)),
            pltpu.SemaphoreType.DMA((2,)),
        ],
        name="build_dense",
        cost_estimate=pl.CostEstimate(
            flops=slots * 128 * 128, bytes_accessed=slots * 128 * 128 * 4, transcendentals=0
        ),
    )(row_index, col_index, count, values)


def body(node_features, weight, cotangent, tile_row, tile_col, tile_values, tile_count):
    rows_here, feature_width = node_features.shape
    dom_size = lax.axis_size("dom")
    rep_size = lax.axis_size("rep")
    slots = tile_row.shape[2]
    row_blocks = rep_size * rows_here // 128
    col_blocks = dom_size * rows_here // 128
    dense = build_dense(
        tile_row.reshape(slots),
        tile_col.reshape(slots),
        tile_count.reshape(1),
        tile_values.reshape(slots, 128, 128),
        row_blocks,
        col_blocks,
    )
    projected = jnp.dot(node_features, weight, preferred_element_type=jnp.float32).astype(jnp.bfloat16)
    source = lax.all_gather(projected, "dom", axis=0, tiled=True)
    partial = jnp.dot(dense, source, preferred_element_type=jnp.float32).astype(jnp.bfloat16)
    pieces = lax.all_to_all(
        partial.reshape(rep_size, rows_here, feature_width), "rep", 0, 0
    )
    summed = jnp.sum(pieces.astype(jnp.float32), axis=0)
    sig = jax.nn.sigmoid(summed)
    output = (summed * sig).astype(jnp.bfloat16)
    slope = sig * (1.0 + summed * (1.0 - sig))
    grad_own = (cotangent.astype(jnp.float32) * slope).astype(jnp.bfloat16)
    grad_block = lax.all_gather(grad_own, "rep", axis=0, tiled=True)
    back = lax.dot_general(
        dense, grad_block, (((0,), (0,)), ((), ())), preferred_element_type=jnp.float32
    ).astype(jnp.bfloat16)
    back_pieces = lax.all_to_all(
        back.reshape(dom_size, rows_here, feature_width), "dom", 0, 0
    )
    grad_projected = jnp.sum(back_pieces.astype(jnp.float32), axis=0).astype(jnp.bfloat16)
    grad_features = jnp.dot(grad_projected, weight.T, preferred_element_type=jnp.float32).astype(
        jnp.bfloat16
    )
    local_weight = jnp.dot(node_features.T, grad_projected, preferred_element_type=jnp.float32)
    grad_weight = lax.psum(local_weight, ("dom", "rep"))
    return (output, grad_features, grad_weight)


def solution(mesh):
    placed = (
        P(("dom", "rep"), None),
        P(),
        P(("dom", "rep"), None),
        P("dom", "rep", None),
        P("dom", "rep", None),
        P("dom", "rep", None, None, None),
        P("dom", "rep"),
    )
    return jax.shard_map(
        body,
        mesh=mesh,
        in_specs=placed,
        out_specs=(P(("dom", "rep"), None), P(("dom", "rep"), None), P()),
        check_vma=False,
    )
```

time: 721 us -> 296 us (0.41)
  other arithmetic: 252 us -> 1.57 us
  waiting for transfers between devices: 250 us -> 158 us
  local copies, waits for them, and re-layouts: 91.8 us -> 2.7 us
  matrix products: 110 us -> 25.8 us
  blocking collectives: 0 us -> 71.5 us
  Pallas kernels: 0 us -> 21.4 us
    scatter-add x8 -> x0, other arithmetic: 248 us -> none  [accumulate(): return summed.at[places].add(products)]
    reduce_scatter x2 -> x0, waiting for transfers between devices: 85.2 us -> none  [the longest x1 50.6 us: body(): lax.psum_scatter(back_partial, 'dom', scatter_dimension=0, tiled=True)]
    dot_general x9 -> x3, matrix products: 106 us -> 23.9 us  [the longest x1 11.1 us: body(): jnp.dot(dense, source, preferred_element_type=jnp.float32)]
    all_to_all x0 -> x2, blocking collectives: none -> 71.5 us  [the longest x1 53.6 us: body(): lax.all_to_all(back.reshape(dom_size, rows_here, feature_width), 'dom', 0...]
    gather x8 -> x0, local copies, waits for them, and re-layouts: 63.7 us -> none  [accumulate(): picked = jnp.take(source, picks, axis=0)]
    all_gather x1, waiting for transfers between devices: 32.9 us -> 9.97 us  [body(): source = lax.all_gather(projected, 'dom', axis=0, tiled=True)]
    unnamed x14 -> x7, local copies, waits for them, and re-layouts: 25.5 us -> 2.7 us
    pallas_call x0 -> x1, Pallas kernels: none -> 21.4 us  [build_dense(): pl.pallas_call(functools.partial(build_kernel, row_blocks, col_blocks), o...]
  transfers between devices with their start and end apart: 5 -> 3, of which waited for: 5 -> 3; matrix products, arithmetic and copies ran while one was open for 3% -> 0% of each run, Pallas kernels for 0% -> 7%
where the time goes in v1:
time: 296 us
  waiting for transfers between devices  158 us (53%)
  blocking collectives  71.5 us (24%)
  matrix products  25.8 us (9%)
  Pallas kernels  21.4 us (7%)
  between operations  14.5 us (5%)
    psum x1, waiting for transfers between devices, body(): grad_weight = lax.psum(local_weight, ('dom', 'rep'))  124 us
    all_to_all x1, blocking collectives, body(): lax.all_to_all(back.reshape(dom_size, rows_here, feature_width), 'dom', 0...  53.6 us
    all_gather x1, waiting for transfers between devices, body(): grad_block = lax.all_gather(grad_own, 'rep', axis=0, tiled=True)  24.5 us
    pallas_call x1, Pallas kernels, build_dense(): pl.pallas_call(functools.partial(build_kernel, row_blocks, col_blocks), o...  21.4 us
    all_to_all x1, blocking collectives, body(): lax.all_to_all(partial.reshape(rep_size, rows_here, feature_width), 'rep'...  18 us
    dot_general x1, matrix products, body(): jnp.dot(dense, source, preferred_element_type=jnp.float32)  11.1 us
    dot_general x1, matrix products, body(): lax.dot_general(dense, grad_block, (((0,), (0,)), ((), ())), preferred_el...  11 us
    all_gather x1, waiting for transfers between devices, body(): source = lax.all_gather(projected, 'dom', axis=0, tiled=True)  9.97 us
  transfers between devices with their start and end apart: 3, of which 3 were waited for; matrix products, arithmetic and copies ran while one was open for 0% of the time, Pallas kernels for 7%

profile of v1, /device:TPU:0, one launch (start us, length us, event | category | flops | bytes accessed | tf_op | source)
XLA Modules:
  0.0 295.8 jit_solution(14559766694531584435)
XLA Ops:
  7.2 0.0 copy-start
  7.2 0.0 all-gather.3.cloned.1.call-start
  7.2 0.9 copy-done
  8.1 1.8 convolution_convert_fusion.3
  9.9 0.0 all-gather.3.cloned.1.call-update
  10.0 0.0 all-gather.5.cloned.1.call-start
  10.7 21.4 %build_dense.1 = bf16[2048,4096]{1,0:T(8,128)(2,1)} custom-call(s32[512]{0:T(512)} %bitcast.22, s32[512]{0:T(512)} %bitcast.23, s32[1]{0:T(128)} %bitcast.18.count_ref, bf16[512,128,128]{2,1,0:T(8,128)(2,1)} %bitcast.19), custom_call_target="tpu_custom_call" | custom-call | flops 8388608 | bytes 33554432 | tf_op jit(solution)/shard_map/build_dense/pallas_call | solution.py:88
  32.1 0.0 copy-start.2
  32.1 10.0 %all-gather.3.cloned.1.call-done = bf16[4096,256]{1,0:T(8,128)(2,1)} async-done(((bf16[512,256]{1,0:T(8,128)(2,1)}), bf16[4096,256]{1,0:T(8,128)(2,1)}) %all-gather.3.cloned.1.call-update) | async-done | bytes 2097168 | tf_op jit(solution)/shard_map/all_gather | solution.py:124
  42.1 11.1 %convolution_convert_fusion.1 = bf16[2048,256]{1,0:T(8,128)(2,1)S(1)} fusion(bf16[2048,4096]{1,0:T(8,128)(2,1)} %build_dense.1, bf16[4096,256]{1,0:T(8,128)(2,1)} %all-gather.3.cloned.1.call-done), kind=kOutput, calls=%fused_computation.1 | convolution fusion | flops 4295491584 | bytes 19922944 | tf_op jit(solution)/shard_map/dot_general | solution.py:125
  53.1 18.0 %all_to_all.10 = bf16[4,512,256]{2,1,0:T(8,128)(2,1)S(1)} all-to-all(bf16[4,512,256]{2,1,0:T(8,128)(2,1)S(1)} %bitcast.21), channel_id=1, replica_groups=mesh['dom'=8,'rep'=4] {'rep'}, dimensions={0} | all-to-all | bytes 2097152 | tf_op jit(solution)/shard_map/all_to_all | solution.py:126
  71.1 0.1 convert_reduce_fusion
  71.2 0.0 copy-done.2
  71.3 1.0 multiply_convert_fusion
  72.3 0.0 all-gather.5.cloned.1.call-update
  72.3 0.0 all-reduce.2.cloned.1.call-start
  72.4 24.5 %all-gather.5.cloned.1.call-done = bf16[2048,256]{1,0:T(8,128)(2,1)} async-done(((bf16[512,256]{1,0:T(8,128)(2,1)}), bf16[2048,256]{1,0:T(8,128)(2,1)}) %all-gather.5.cloned.1.call-update) | async-done | bytes 1048592 | tf_op jit(solution)/shard_map/all_gather | solution.py:134
  96.9 11.0 %convolution_convert_fusion = bf16[4096,256]{1,0:T(8,128)(2,1)S(1)} fusion(bf16[2048,4096]{1,0:T(8,128)(2,1)} %build_dense.1, bf16[2048,256]{1,0:T(8,128)(2,1)} %all-gather.5.cloned.1.call-done), kind=kOutput, calls=%fused_computation | convolution fusion | flops 4296015872 | bytes 19922944 | tf_op jit(solution)/shard_map/dot_general | solution.py:135
  107.9 0.0 copy-start.1
  107.9 53.6 %all_to_all.11 = bf16[8,512,256]{2,1,0:T(8,128)(2,1)S(1)} all-to-all(bf16[8,512,256]{2,1,0:T(8,128)(2,1)S(1)} %bitcast.20), channel_id=1, replica_groups=mesh['dom'=8,'rep'=4] {'dom'}, dimensions={0} | all-to-all | bytes 4194304 | tf_op jit(solution)/shard_map/all_to_all | solution.py:138
  161.5 0.4 reduce_sum.22
  161.9 1.0 convolution_bitcast_fusion
  162.9 0.0 all-reduce.2.cloned.1.call-update
  162.9 0.0 copy-done.1
  162.9 1.0 convolution_convert_fusion.2
  163.9 123.7 %all-reduce.2.cloned.1.call-done = f32[256,256]{0,1:T(8,128)} async-done(((f32[256,256]{0,1:T(8,128)}), f32[256,256]{0,1:T(8,128)}) %all-reduce.2.cloned.1.call-update) | async-done | bytes 262160 | tf_op jit(solution)/shard_map/psum | solution.py:146
  287.5 1.8 copy.10
Async XLA Ops:
  7.2 1.0 copy-start
  7.2 34.9 %all-gather.3.cloned.1.call-start = ((), (), s32[]{:S(2)}) async-start(), calls=%async_computation.2 | async-start | bytes 2359296 | tf_op jit(solution)/shard_map/all_gather | solution.py:124
  10.0 86.9 %all-gather.5.cloned.1.call-start = ((), (), s32[]{:S(2)}) async-start(), calls=%async_computation.3 | async-start | bytes 1310720 | tf_op jit(solution)/shard_map/all_gather | solution.py:134
  32.1 39.1 %copy-start.2 = (bf16[512,256]{1,0:T(8,128)(2,1)S(1)}, bf16[512,256]{1,0:T(8,128)(2,1)}, u32[]{:S(2)}) copy-start(bf16[512,256]{1,0:T(8,128)(2,1)} %param.9) | copy-start | bytes 786436
  72.3 215.2 %all-reduce.2.cloned.1.call-start = ((), (), s32[]{:S(2)}) async-start(), calls=%async_computation.4 | async-start | bytes 524288 | tf_op jit(solution)/shard_map/psum | solution.py:146
  107.9 55.0 %copy-start.1 = (bf16[256,256]{1,0:T(8,128)(2,1)S(1)}, bf16[256,256]{1,0:T(8,128)(2,1)}, u32[]{:S(2)}) copy-start(bf16[256,256]{1,0:T(8,128)(2,1)} %param.8) | copy-start | bytes 393220
Sparse Core Ops, SparseCore 0:
  10.2 31.8 all-gather.2
  72.4 24.4 all-gather.4
  163.0 124.4 all-reduce.1
